TPU v7x, 32 devices: a whole 2x2x4 slice. The times are simulated.
32 devices in a mesh: req: 16 (over z, y, core), tp: 2 (over x).
Axes of the slice: x: 2, y: 2, z: 4, core: 2. Of those that a mesh axis runs over, the one named last changes fastest.
Arguments:
- queries: bfloat16 [1024, 2048], P('req', 'tp'), may hold values from -18 to 18
- fresh_key_value: bfloat16 [1024, 1024], P('req', 'tp'), may hold values from -6 to 6
- key_value_cache: bfloat16 [64, 128, 1024], P('req', None, 'tp'), may hold values from -12.2 to 12.2
- request_page_index: int32 [144, 4], P('req'), may hold values from 0 to 3
- cache_length_rows: int32 [144], P('req'), may hold values from 2 to 512, as said below
- residual: bfloat16 [1024, 2048], P('req'), may hold values from -12.8 to 12.8
- w_out: bfloat16 [2048, 2048], P('tp'), may hold values from -0.125 to 0.125
- gain_in: float32 [2048], replicated, may hold values from 0.5 to 1.5
- route_ids: int32 [1024, 8], P('req'), may hold values from 0 to 15, all different within a row; in each aligned block of 32 rows (0 to 31, 32 to 63, ...) at most 32 rows name the same one
- route_weights: float32 [1024, 8], P('req'), may hold values from 0.1 to 1
- expert_home: int32 [16], replicated, may hold values from 0 to 15, each once
- w_gate: bfloat16 [16, 2048, 768], P('req', None, 'tp'), may hold values from -0.125 to 0.125
- w_up: bfloat16 [16, 2048, 768], P('req', None, 'tp'), may hold values from -0.125 to 0.125
- w_down: bfloat16 [16, 768, 2048], P('req', 'tp'), may hold values from -0.21875 to 0.21875
- gain_out: float32 [2048], replicated, may hold values from 0.5 to 1.5
Outputs:
- normed: bfloat16 [1024, 2048], P(('req', 'tp'))
Inputs may be any that keep to these rules, and one draw needn't show every extreme that they name: `route_ids`: each row names 8 different experts; in each aligned block of 32 rows no expert is named by more than 32 rows, and in some block some expert by exactly 32. `expert_home`: each expert is held by exactly one group. `request_page_index`: entries number pages among the 4 pages of the request's own group; a page may be named by several requests and entries. `cache_length_rows`: in every group one request has exactly 512 cached tokens.
All inputs are finite; a program needn't handle non-finite values.
Results may differ from a plain program's by a relative error of at most 0.0058.
Values may be sent and summed in bfloat16 or wider, within the bound.
No kernel may reach another device: no remote copies, remote signals or barrier semaphores. Data moves between devices by JAX's collectives and lax.ppermute only.
A program may use at most 64 MiB of HBM per device.

v0:
```python
import jax
import jax.numpy as jnp
from jax import lax
from jax.sharding import PartitionSpec as P

HEAD_WIDTH = 128
TOPK = 8
PRE_DEV = 56
EPSILON = 1e-06


def rms_scale(value_rows, gain_row):
    mean_square = jnp.mean(value_rows * value_rows, axis=-1, keepdims=True)
    return value_rows * lax.rsqrt(mean_square + EPSILON) * gain_row


def softmax_rounded(scores):
    row_peak = jnp.max(scores, axis=-1, keepdims=True)
    weights = jnp.exp(scores - row_peak)
    return (weights / jnp.sum(weights, axis=-1, keepdims=True)).astype(jnp.bfloat16)


def group_attention(queries, fresh_key_value, page_pool, page_rows, lengths):
    tokens_here = queries.shape[0]
    kv_heads = fresh_key_value.shape[1] // (2 * HEAD_WIDTH)
    group_size = queries.shape[1] // (HEAD_WIDTH * kv_heads)
    score_scale = HEAD_WIDTH ** (-0.5)
    split_query = queries.reshape(tokens_here, kv_heads, group_size, HEAD_WIDTH)
    fresh_kv = fresh_key_value.reshape(tokens_here, kv_heads, 2, HEAD_WIDTH)
    gathered_pages = page_pool[page_rows]
    cached = gathered_pages.reshape(page_rows.shape[0], -1, kv_heads, 2, HEAD_WIDTH)
    places = jnp.arange(cached.shape[1], dtype=jnp.int32)
    prefill_query = split_query[:PRE_DEV]
    prefill_fresh = fresh_kv[:PRE_DEV]
    cache_scores = (
        jnp.einsum(
            "ikgd,ckd->kgic", prefill_query, cached[0, :, :, 0], preferred_element_type=jnp.float32
        )
        * score_scale
    )
    cache_scores = jnp.where(places < lengths[0], cache_scores, -jnp.inf)
    block_scores = (
        jnp.einsum(
            "ikgd,jkd->kgij",
            prefill_query,
            prefill_fresh[:, :, 0],
            preferred_element_type=jnp.float32,
        )
        * score_scale
    )
    causal = jnp.arange(PRE_DEV)[:, None] >= jnp.arange(PRE_DEV)[None, :]
    block_scores = jnp.where(causal, block_scores, -jnp.inf)
    prefill_probs = softmax_rounded(jnp.concatenate([cache_scores, block_scores], axis=3))
    prefill_values = jnp.concatenate([cached[0, :, :, 1], prefill_fresh[:, :, 1]], axis=0)
    prefill_out = jnp.einsum(
        "kgic,ckd->ikgd", prefill_probs, prefill_values, preferred_element_type=jnp.float32
    )
    decode_query = split_query[PRE_DEV:]
    decode_fresh = fresh_kv[PRE_DEV:]
    decode_scores = (
        jnp.einsum(
            "rkgd,rckd->rkgc", decode_query, cached[1:, :, :, 0], preferred_element_type=jnp.float32
        )
        * score_scale
    )
    decode_scores = jnp.where(
        places[None, None, None, :] < lengths[1:, None, None, None], decode_scores, -jnp.inf
    )
    own_scores = (
        jnp.einsum(
            "rkgd,rkd->rkg", decode_query, decode_fresh[:, :, 0], preferred_element_type=jnp.float32
        )[..., None]
        * score_scale
    )
    decode_probs = softmax_rounded(jnp.concatenate([decode_scores, own_scores], axis=3))
    decode_values = jnp.concatenate([cached[1:, :, :, 1], decode_fresh[:, None, :, 1]], axis=1)
    decode_out = jnp.einsum(
        "rkgc,rckd->rkgd", decode_probs, decode_values, preferred_element_type=jnp.float32
    )
    joined = jnp.concatenate([prefill_out, decode_out], axis=0)
    return joined.reshape(tokens_here, -1).astype(jnp.bfloat16)


def slot_positions(block_owner, experts, capacity):
    flat_owner = block_owner.reshape(-1)
    onehot = (flat_owner[:, None] == jnp.arange(experts, dtype=jnp.int32)[None, :]).astype(
        jnp.int32
    )
    earlier = jnp.cumsum(onehot, axis=0) - onehot
    slot_index = jnp.sum(earlier * onehot, axis=1)
    return (flat_owner * capacity + slot_index).reshape(block_owner.shape)


def place_matrix(positions, slots_total):
    matches = positions[None, :, :] == jnp.arange(slots_total, dtype=jnp.int32)[:, None, None]
    return jnp.any(matches, axis=2).astype(jnp.bfloat16)


def local(
    queries,
    fresh_key_value,
    key_value_cache,
    request_page_index,
    cache_length_rows,
    residual,
    w_out,
    gain_in,
    route_ids,
    route_weights,
    expert_home,
    w_gate,
    w_up,
    w_down,
    gain_out,
):
    tp_size = lax.axis_size("tp")
    req_size = lax.axis_size("req")
    tp_index = lax.axis_index("tp")
    model_width = residual.shape[1]
    tokens_here = residual.shape[0]
    quarter = tokens_here // tp_size
    experts = expert_home.shape[0]
    capacity = min(quarter, max(2, 2 * quarter * TOPK // experts))
    context = group_attention(
        queries, fresh_key_value, key_value_cache, request_page_index, cache_length_rows
    )
    head_terms = jnp.dot(context, w_out, preferred_element_type=jnp.float32)
    state = residual.astype(jnp.float32) + lax.psum(head_terms, "tp")
    owners = jnp.sum(
        jnp.where(
            route_ids[:, :, None] == jnp.arange(experts, dtype=jnp.int32)[None, None, :],
            expert_home[None, None, :],
            0,
        ),
        axis=2,
    )
    shares = route_weights / jnp.sum(route_weights, axis=1, keepdims=True)
    own_start = tp_index * quarter
    own_state = lax.dynamic_slice_in_dim(state, own_start, quarter, 0)
    own_shares = lax.dynamic_slice_in_dim(shares, own_start, quarter, 0)
    normed_all = rms_scale(state, gain_in).astype(jnp.bfloat16)
    positions_all = jax.vmap(lambda block_owner: slot_positions(block_owner, experts, capacity))(
        owners.reshape(tp_size, quarter, TOPK)
    )
    placing = jax.vmap(lambda positions: place_matrix(positions, experts * capacity))(positions_all)
    outgoing = jnp.einsum(
        "qmi,qid->qmd",
        placing,
        normed_all.reshape(tp_size, quarter, model_width),
        preferred_element_type=jnp.float32,
    )
    outgoing = outgoing.astype(jnp.bfloat16).reshape(tp_size, experts, capacity, model_width)
    incoming = lax.all_to_all(outgoing, "req", split_axis=1, concat_axis=1, tiled=True)
    own_positions = lax.dynamic_index_in_dim(positions_all, tp_index, 0, keepdims=False)
    expert_rows = incoming.reshape(-1, model_width)
    gate_proj = jnp.dot(expert_rows, w_gate[0], preferred_element_type=jnp.float32)
    up_proj = jnp.dot(expert_rows, w_up[0], preferred_element_type=jnp.float32)
    inner_units = (jax.nn.silu(gate_proj) * up_proj).astype(jnp.bfloat16)
    summed = lax.psum_scatter(
        jnp.dot(inner_units, w_down[0], preferred_element_type=jnp.float32).astype(jnp.bfloat16),
        "tp",
        scatter_dimension=0,
        tiled=True,
    )
    results = summed.reshape(req_size, capacity, model_width)
    returned = lax.all_to_all(results, "req", split_axis=0, concat_axis=0, tiled=True).reshape(
        -1, model_width
    )
    picked = returned[own_positions]
    mixture = jnp.sum(own_shares[:, :, None] * picked.astype(jnp.float32), axis=1)
    return rms_scale(own_state + mixture, gain_out).astype(jnp.bfloat16)


def solution(mesh):
    return jax.shard_map(
        local,
        mesh=mesh,
        in_specs=(
            P("req", "tp"),
            P("req", "tp"),
            P("req", None, "tp"),
            P("req", None),
            P("req"),
            P("req", None),
            P("tp", None),
            P(),
            P("req", None),
            P("req", None),
            P(),
            P("req", None, "tp"),
            P("req", None, "tp"),
            P("req", "tp", None),
            P(),
        ),
        out_specs=P(("req", "tp"), None),
        check_vma=False,
    )
```

profile of v0, /device:TPU:13, one launch (start us, length us, event | category | flops | bytes accessed | tf_op | source)
XLA Modules:
  0.0 313.9 jit_solution(11618750523219073472)
XLA Ops:
  6.5 0.8 compare_select_fusion.1
  7.3 0.1 copy.76
  7.5 5.4 %gather_fusion = bf16[36,128,512]{2,1,0:T(8,128)(2,1)} fusion(bf16[4,128,512]{2,1,0:T(8,128)(2,1)} %param.17, s32[1024]{0:T(1024)S(1)} %pad_clamp_fusion.1), kind=kCustom, calls=%fused_computation | custom fusion | bytes 9437328 | tf_op jit(solution)/shard_map/gather | solution.py:30
  13.0 7.7 %reshape.139 = bf16[9,512,2,2,128]{4,3,2,1,0:T(2,128)(2,1)} reshape(bf16[36,128,512]{2,1,0:T(8,128)(2,1)} %gather_fusion) | data formatting | bytes 9437184 | tf_op jit(solution)/shard_map/reshape | solution.py:31
  20.7 10.0 %fusion.46 = (bf16[8,512,2,1,128]{4,3,2,1,0:T(2,128)(2,1)}, bf16[8,512,2,1,128]{4,3,2,1,0:T(2,128)(2,1)}) fusion(bf16[9,512,2,2,128]{4,3,2,1,0:T(2,128)(2,1)} %reshape.139), kind=kLoop, calls=%fused_computation.93 | loop fusion | bytes 8388608 | tf_op jit(solution)/shard_map/slice | solution.py:62
  30.7 2.1 fusion.45
  33.1 0.1 fusion.38
  33.2 2.9 fusion.48
  36.2 0.2 copy.85
  36.4 2.7 copy.146
  39.1 0.2 fusion.33
  39.4 0.5 fusion
  39.9 0.4 slice-done.1
  40.4 0.1 fusion.47
  40.5 0.4 fusion.49
  40.9 0.3 fusion.50
  41.3 0.3 fusion.23
  41.6 0.5 fusion.21
  42.1 0.1 copy.89
  42.3 3.9 %fusion.51 = f32[64,2048]{1,0:T(8,128)} fusion(bf16[64,1024]{1,0:T(8,128)(2,1)S(1)} %convert_element_type.42, bf16[1024,2048]{1,0:T(8,128)(2,1)} %param.21), kind=kOutput, calls=%fused_computation.98 | convolution fusion | flops 268435456 | bytes 4849664 | tf_op jit(solution)/shard_map/dot_general | solution.py:127
  46.3 0.1 select_reduce_fusion
  46.4 0.1 copy.91
  46.5 0.1 eq.58
  46.6 1.2 reduce-window.6
  47.7 0.2 slice_reduce_fusion
  47.9 0.1 eq.54
  48.1 0.1 fusion.36
  48.2 0.1 reduce_sum.79
  48.3 0.1 copy.104
  48.4 0.4 fusion.22
  48.8 27.4 %all-reduce.2.cloned.1.call-done = f32[64,2048]{1,0:T(8,128)} async-done(((f32[64,2048]{1,0:T(8,128)}), f32[64,2048]{1,0:T(8,128)}) %all-reduce.2.cloned.1.call-update) | async-done | bytes 524304 | tf_op jit(solution)/shard_map/psum | solution.py:128
  76.1 1.2 multiply_reduce_fusion
  77.4 0.1 multiply_convert_fusion.1
  77.5 1.3 convolution_convert_fusion.1
  78.8 0.6 copy.95
  79.4 98.4 %all_to_all.10 = bf16[2,16,32,2048]{3,2,0,1:T(8,128)(2,1)S(1)} all-to-all(bf16[2,16,32,2048]{3,2,0,1:T(8,128)(2,1)S(1)} %copy.95), channel_id=1, replica_groups=mesh['req'=16,'tp'=2] {'req'}, dimensions={1} | all-to-all | bytes 8388608 | tf_op jit(solution)/shard_map/all_to_all | solution.py:153
  177.8 0.6 copy.96
  178.4 2.0 copy-done.1
  180.3 3.6 %fusion.9 = f32[1024,384]{1,0:T(8,128)} fusion(bf16[1024,2048]{1,0:T(8,128)(2,1)S(1)} %bitcast.118, bf16[1,2048,384]{2,1,0:T(8,128)(2,1)S(1)} %copy-done.8), kind=kOutput, calls=%fused_computation.16 | convolution fusion | flops 1610612736 | bytes 7340032 | tf_op jit(solution)/shard_map/dot_general | solution.py:156
  183.9 9.6 %convolution_convert_fusion = bf16[1024,2048]{1,0:T(8,128)(2,1)} fusion(bf16[1,384,2048]{2,1,0:T(8,128)(2,1)S(1)} %copy-done, f32[1024,384]{1,0:T(8,128)} %fusion.9, bf16[1024,2048]{1,0:T(8,128)(2,1)} %bitcast.119, bf16[1,2048,384]{2,1,0:T(8,128)(2,1)} %param.27), kind=kOutput, calls=%fused_computation.2 | convolution fusion | flops 3225681920 | bytes 13107200 | tf_op jit(solution)/shard_map/dot_general | solution.py:160
  193.5 53.4 %reduce-scatter.2.cloned.1.call-done = bf16[512,2048]{1,0:T(8,128)(2,1)} async-done(((bf16[1024,2048]{1,0:T(8,128)(2,1)}), bf16[512,2048]{1,0:T(8,128)(2,1)}) %reduce-scatter.2.cloned.1.call-update) | async-done | bytes 2097168 | tf_op jit(solution)/shard_map/reduce_scatter | solution.py:159
  246.9 6.5 %all-to-all-start.1 = ((bf16[16,32,2048]{2,1,0:T(8,128)(2,1)}), bf16[16,32,2048]{2,1,0:T(8,128)(2,1)}, u32[]{:S(2)}, u32[]{:S(2)}) async-start(bf16[16,32,2048]{2,1,0:T(8,128)(2,1)} %bitcast.121), calls=%async_computation.2 | async-start | bytes 4194304 | tf_op jit(solution)/shard_map/all_to_all | solution.py:166
  253.4 0.1 reshape.156
  253.7 47.2 %all-to-all-done.1 = bf16[16,32,2048]{2,1,0:T(8,128)(2,1)} async-done(((bf16[16,32,2048]{2,1,0:T(8,128)(2,1)}), bf16[16,32,2048]{2,1,0:T(8,128)(2,1)}, u32[]{:S(2)}, u32[]{:S(2)}) %all-to-all-start.1) | async-done | bytes 2097184 | tf_op jit(solution)/shard_map/all_to_all | solution.py:166
  300.9 4.2 %gather_fusion.1 = bf16[256,2048]{1,0:T(8,128)(2,1)S(1)} fusion(bf16[512,2048]{1,0:T(8,128)(2,1)} %bitcast.33, s32[1024]{0:T(1024)S(1)} %pad_clamp_fusion), kind=kCustom, calls=%fused_computation.1 | custom fusion | bytes 2098176 | tf_op jit(solution)/shard_map/gather | solution.py:169
  305.2 1.0 fusion.5
  306.2 0.2 multiply_reduce_fusion.1
  306.3 0.8 multiply_convert_fusion.2
  (61 shorter events, 1.0 us)
Async XLA Ops:
  6.5 177.4 %copy-start = (bf16[1,384,2048]{2,1,0:T(8,128)(2,1)S(1)}, bf16[1,384,2048]{2,1,0:T(8,128)(2,1)}, u32[]{:S(2)}) copy-start(bf16[1,384,2048]{2,1,0:T(8,128)(2,1)} %param.28) | copy-start | bytes 4718596
  6.5 69.6 %all-reduce.2.cloned.1.call-start = ((), (), s32[]{:S(2)}) async-start(), calls=%async_computation.3 | async-start | bytes 1048576 | tf_op jit(solution)/shard_map/psum | solution.py:128
  30.7 2.2 slice-start
  30.7 2.2 copy-start.9
  30.7 2.3 slice-start.2
  39.3 0.9 slice-start.1
  39.3 1.0 slice-start.3
  42.3 4.0 %copy-start.6 = (s32[64,8]{0,1:T(8,128)S(1)}, s32[64,8]{0,1:T(8,128)}, u32[]{:S(2)}) copy-start(s32[64,8]{0,1:T(8,128)} %param.23) | copy-start | bytes 6148
  42.3 4.0 %copy-start.7 = (s32[16]{0:T(128)S(1)}, s32[16]{0:T(128)}, u32[]{:S(2)}) copy-start(s32[16]{0:T(128)} %param.25) | copy-start | bytes 196
  42.3 33.8 %copy-start.2 = (bf16[64,2048]{1,0:T(8,128)(2,1)S(1)}, bf16[64,2048]{1,0:T(8,128)(2,1)}, u32[]{:S(2)}) copy-start(bf16[64,2048]{1,0:T(8,128)(2,1)} %param.20) | copy-start | bytes 786436
  46.2 31.2 %copy-start.4 = (f32[2048]{0:T(1024)S(1)}, f32[2048]{0:T(1024)}, u32[]{:S(2)}) copy-start(f32[2048]{0:T(1024)} %param.22) | copy-start | bytes 24580
  46.2 200.7 %reduce-scatter.2.cloned.1.call-start = ((), (), s32[]{:S(2)}) async-start(), calls=%async_computation.4 | async-start | bytes 6291456 | tf_op jit(solution)/shard_map/reduce_scatter | solution.py:159
  177.8 2.6 copy-start.8
  178.4 2.0 copy-start.1
  246.9 6.6 %copy-start.3 = (f32[64,8]{0,1:T(8,128)S(1)}, f32[64,8]{0,1:T(8,128)}, u32[]{:S(2)}) copy-start(f32[64,8]{0,1:T(8,128)} %param.24) | copy-start | bytes 6148
  246.9 54.0 %all-to-all-start.1 = ((bf16[16,32,2048]{2,1,0:T(8,128)(2,1)}), bf16[16,32,2048]{2,1,0:T(8,128)(2,1)}, u32[]{:S(2)}, u32[]{:S(2)}) async-start(bf16[16,32,2048]{2,1,0:T(8,128)(2,1)} %bitcast.121), calls=%async_computation.2 | async-start | bytes 4194304 | tf_op jit(solution)/shard_map/all_to_all | solution.py:166
  300.9 5.4 %copy-start.5 = (f32[2048]{0:T(1024)S(1)}, f32[2048]{0:T(1024)}, u32[]{:S(2)}) copy-start(f32[2048]{0:T(1024)} %param.29) | copy-start | bytes 24580
Sparse Core Ops, SparseCore 0:
  46.3 29.7 all-reduce.1
  193.6 53.2 reduce-scatter.1
where the time goes:
time: 315 us; the launch traced here: 314 us
  waiting for transfers between devices  128 us (41%)
  blocking collectives  98.4 us (31%)
  local copies, waits for them, and re-layouts  37.6 us (12%)
  matrix products  23 us (7%)
  between operations  13.8 us (4%)
  starting transfers between devices  6.55 us (2%)
  other arithmetic  6.54 us (2%)
    all_to_all x1, blocking collectives, local(): lax.all_to_all(outgoing, 'req', split_axis=1, concat_axis=1, tiled=True)  98.4 us
    reduce_scatter x1, waiting for transfers between devices, local(): lax.psum_scatter(jnp.dot(inner_units, w_down[0], preferred_element_type=j...  53.4 us
    all_to_all x1, waiting for transfers between devices, local(): lax.all_to_all(results, 'req', split_axis=0, concat_axis=0, tiled=True)  47.2 us
    psum x1, waiting for transfers between devices, local(): state = residual.astype(jnp.float32) + lax.psum(head_terms, 'tp')  27.4 us
    slice x1, local copies, waits for them, and re-layouts, group_attention(): cached[1:, :, :, 0]  10 us
    dot_general x1, matrix products, local(): jnp.dot(inner_units, w_down[0], preferred_element_type=jnp.float32)  9.56 us
    reshape x1, local copies, waits for them, and re-layouts, group_attention(): gathered_pages.reshape(page_rows.shape[0], -1, kv_heads, 2, HEAD_WIDTH)  7.7 us
    all_to_all x1, starting transfers between devices, local(): lax.all_to_all(results, 'req', split_axis=0, concat_axis=0, tiled=True)  6.5 us
  transfers between devices with their start and end apart: 3, of which 3 were waited for; matrix products, arithmetic and copies ran while one was open for 1% of the time, Pallas kernels for 0%

commit v1 on v0

--- a/solution.py
+++ b/solution.py
@@ -7,6 +7,20 @@
 TOPK = 8
 PRE_DEV = 56
 EPSILON = 1e-06
+
+
+def _cover_zone(vec, d_out, block_here):
+    mixed_arr = vec.shape
+    side_arr = vec.reshape(
+        *mixed_arr[:d_out], block_here, mixed_arr[d_out] // block_here, *mixed_arr[d_out + 1 :]
+    )
+    return jnp.moveaxis(side_arr, d_out, 0)
+
+
+def apply_node(q_in, row_dim):
+    big = list(q_in.shape[1:])
+    big[row_dim] *= q_in.shape[0]
+    return jnp.moveaxis(q_in, 0, row_dim).reshape(big)
 
 
 def rms_scale(value_rows, gain_row):
@@ -163,9 +177,18 @@
         tiled=True,
     )
     results = summed.reshape(req_size, capacity, model_width)
-    returned = lax.all_to_all(results, "req", split_axis=0, concat_axis=0, tiled=True).reshape(
-        -1, model_width
-    )
+
+    def keep_up_frame_over_axis(z, mesh_ax, array_in, piece_in):
+        tall, newest = (lax.axis_size(mesh_ax), lax.axis_index(mesh_ax))
+        s_next = _cover_zone(z, array_in, tall)
+        line_up = [s_next[newest]]
+        for w in tuple(range(1, tall)):
+            kept_arr = s_next[newest ^ w]
+            line_up.append(lax.ppermute(kept_arr, mesh_ax, [(t, t ^ w) for t in range(tall)]))
+        s_next = jnp.stack(line_up, axis=0)[newest ^ jnp.arange(tall)]
+        return apply_node(s_next, piece_in)
+
+    returned = keep_up_frame_over_axis(results, "req", 0, 0).reshape(-1, model_width)
     picked = returned[own_positions]
     mixture = jnp.sum(own_shares[:, :, None] * picked.astype(jnp.float32), axis=1)
     return rms_scale(own_state + mixture, gain_out).astype(jnp.bfloat16)

time: 315 us -> 328 us (1.041)
  waiting for transfers between devices: 128 us -> 110 us
  local copies, waits for them, and re-layouts: 37.6 us -> 54.6 us
  starting transfers between devices: 6.55 us -> 19.5 us
    all_to_all x1 -> x0, waiting for transfers between devices: 47.2 us -> none  [local(): lax.all_to_all(results, 'req', split_axis=0, concat_axis=0, tiled=True)]
    ppermute x0 -> x15, waiting for transfers between devices: none -> 27.5 us  [keep_up_frame_over_axis(): lax.ppermute(kept_arr, mesh_ax, [(t, t ^ w) for t in range(tall)])]
    ppermute x0 -> x15, starting transfers between devices: none -> 19.5 us  [keep_up_frame_over_axis(): lax.ppermute(kept_arr, mesh_ax, [(t, t ^ w) for t in range(tall)])]
    unnamed x23 -> x37, local copies, waits for them, and re-layouts: 4.77 us -> 15.4 us
    all_to_all x1 -> x0, starting transfers between devices: 6.5 us -> none  [local(): lax.all_to_all(results, 'req', split_axis=0, concat_axis=0, tiled=True)]
    gather x0 -> x1, local copies, waits for them, and re-layouts: none -> 3.56 us  [keep_up_frame_over_axis(): s_next = jnp.stack(line_up, axis=0)[newest ^ jnp.arange(tall)]]
  transfers between devices with their start and end apart: 3 -> 17, of which waited for: 3 -> 10; matrix products, arithmetic and copies ran while one was open for 1% -> 3% of each run, Pallas kernels for 0% -> 0%
where the time goes in v1:
time: 328 us; the launch traced here: 326 us
  waiting for transfers between devices  110 us (34%)
  blocking collectives  98.4 us (30%)
  local copies, waits for them, and re-layouts  54.6 us (17%)
  matrix products  23 us (7%)
  starting transfers between devices  19.5 us (6%)
  between operations  13.9 us (4%)
  other arithmetic  7.29 us (2%)
    all_to_all x1, blocking collectives, local(): lax.all_to_all(outgoing, 'req', split_axis=1, concat_axis=1, tiled=True)  98.4 us
    reduce_scatter x1, waiting for transfers between devices, local(): lax.psum_scatter(jnp.dot(inner_units, w_down[0], preferred_element_type=j...  52.6 us
    psum x1, waiting for transfers between devices, local(): state = residual.astype(jnp.float32) + lax.psum(head_terms, 'tp')  29.4 us
    ppermute x15, waiting for transfers between devices, keep_up_frame_over_axis(): lax.ppermute(kept_arr, mesh_ax, [(t, t ^ w) for t in range(tall)])  27.5 us
    ppermute x15, starting transfers between devices, keep_up_frame_over_axis(): lax.ppermute(kept_arr, mesh_ax, [(t, t ^ w) for t in range(tall)])  19.5 us
    unnamed x37, local copies, waits for them, and re-layouts  15.4 us
    slice x1, local copies, waits for them, and re-layouts, group_attention(): cached[1:, :, :, 0]  10 us
    dot_general x1, matrix products, local(): jnp.dot(inner_units, w_down[0], preferred_element_type=jnp.float32)  9.56 us
  transfers between devices with their start and end apart: 17, of which 10 were waited for; matrix products, arithmetic and copies ran while one was open for 3% of the time, Pallas kernels for 0%

profile of v1, /device:TPU:13, one launch (start us, length us, event | category | flops | bytes accessed | tf_op | source)
XLA Modules:
  0.0 326.2 jit_solution(6025311248421793141)
XLA Ops:
  6.5 0.9 select_reduce_fusion
  7.8 1.2 reduce-window.6
  9.6 0.7 compare_select_fusion.1
  10.5 4.4 %gather_fusion = bf16[36,128,512]{2,1,0:T(8,128)(2,1)} fusion(bf16[4,128,512]{2,1,0:T(8,128)(2,1)S(1)} %copy-done.1, s32[1024]{0:T(1024)S(1)} %get-tuple-element.40), kind=kCustom, calls=%fused_computation | custom fusion | bytes 9437328 | tf_op jit(solution)/shard_map/gather | solution.py:44
  14.9 7.7 %reshape.149 = bf16[9,512,2,2,128]{4,3,2,1,0:T(2,128)(2,1)} reshape(bf16[36,128,512]{2,1,0:T(8,128)(2,1)} %gather_fusion) | data formatting | bytes 9437184 | tf_op jit(solution)/shard_map/reshape | solution.py:45
  22.6 10.0 %fusion.47 = (bf16[8,512,2,1,128]{4,3,2,1,0:T(2,128)(2,1)}, bf16[8,512,2,1,128]{4,3,2,1,0:T(2,128)(2,1)}) fusion(bf16[9,512,2,2,128]{4,3,2,1,0:T(2,128)(2,1)} %reshape.149), kind=kLoop, calls=%fused_computation.128 | loop fusion | bytes 8388608 | tf_op jit(solution)/shard_map/slice | solution.py:76
  32.7 2.1 fusion.46
  35.1 2.9 fusion.49
  38.3 2.7 copy.146
  44.2 3.9 %fusion.52 = f32[64,2048]{1,0:T(8,128)} fusion(bf16[64,1024]{1,0:T(8,128)(2,1)S(1)} %convert_element_type.42, bf16[1024,2048]{1,0:T(8,128)(2,1)} %param.21), kind=kOutput, calls=%fused_computation.133 | convolution fusion | flops 268435456 | bytes 4849664 | tf_op jit(solution)/shard_map/dot_general | solution.py:141
  48.5 29.4 %all-reduce.2.cloned.1.call-done = f32[64,2048]{1,0:T(8,128)} async-done(((f32[64,2048]{1,0:T(8,128)}), f32[64,2048]{1,0:T(8,128)}) %all-reduce.2.cloned.1.call-update) | async-done | bytes 524304 | tf_op jit(solution)/shard_map/psum | solution.py:142
  78.0 1.2 multiply_reduce_fusion
  79.3 1.3 convolution_convert_fusion.1
  81.2 98.4 %all_to_all.5 = bf16[2,16,32,2048]{3,2,0,1:T(8,128)(2,1)S(1)} all-to-all(bf16[2,16,32,2048]{3,2,0,1:T(8,128)(2,1)S(1)} %copy.95), channel_id=1, replica_groups=mesh['req'=16,'tp'=2] {'req'}, dimensions={1} | all-to-all | bytes 8388608 | tf_op jit(solution)/shard_map/all_to_all | solution.py:167
  180.2 2.0 copy-done.2
  182.2 3.6 %fusion.9 = f32[1024,384]{1,0:T(8,128)} fusion(bf16[1024,2048]{1,0:T(8,128)(2,1)S(1)} %bitcast.182, bf16[1,2048,384]{2,1,0:T(8,128)(2,1)S(1)} %copy-done.8), kind=kOutput, calls=%fused_computation.17 | convolution fusion | flops 1610612736 | bytes 7340032 | tf_op jit(solution)/shard_map/dot_general | solution.py:170
  185.7 9.6 %convolution_convert_fusion = bf16[1024,2048]{1,0:T(8,128)(2,1)} fusion(bf16[1,384,2048]{2,1,0:T(8,128)(2,1)S(1)} %copy-done, f32[1024,384]{1,0:T(8,128)} %fusion.9, bf16[1024,2048]{1,0:T(8,128)(2,1)} %bitcast.183, bf16[1,2048,384]{2,1,0:T(8,128)(2,1)} %param.27), kind=kOutput, calls=%fused_computation.3 | convolution fusion | flops 3225681920 | bytes 13107200 | tf_op jit(solution)/shard_map/dot_general | solution.py:174
  196.1 52.6 %reduce-scatter.2.cloned.1.call-done = bf16[512,2048]{1,0:T(8,128)(2,1)} async-done(((bf16[1024,2048]{1,0:T(8,128)(2,1)}), bf16[512,2048]{1,0:T(8,128)(2,1)}) %reduce-scatter.2.cloned.1.call-update) | async-done | bytes 2097168 | tf_op jit(solution)/shard_map/reduce_scatter | solution.py:173
  248.7 2.5 dynamic-slice_bitcast_fusion
  251.2 0.7 collective-permute-start
  251.9 0.7 copy.90
  252.8 1.4 collective-permute-start.2
  254.5 1.6 collective-permute-start.4
  256.3 1.6 bitcast_dynamic-update-slice_fusion.14
  257.9 2.3 collective-permute-start.6
  260.2 0.7 bitcast_dynamic-update-slice_fusion.13
  261.1 2.1 collective-permute-start.7
  263.2 0.7 bitcast_dynamic-update-slice_fusion.12
  264.3 0.7 bitcast_dynamic-update-slice_fusion.11
  265.0 2.1 collective-permute-start.9
  267.7 5.5 %collective-permute-start.10 = (bf16[1,32,2048]{2,1,0:T(8,128)(2,1)S(1)}, bf16[1,32,2048]{2,1,0:T(8,128)(2,1)S(1)}, u32[]{:S(2)}, u32[]{:S(2)}) collective-permute-start(bf16[1,32,2048]{2,1,0:T(8,128)(2,1)S(1)} %get-tuple-element.15), channel_id=1, source_target_pairs={{0,22},{2,20},{4,18},{6,16},{8,30},{10,28},{12,26},{14,24},{16,6},... | collective-permute-start | bytes 393224 | tf_op jit(solution)/shard_map/ppermute | solution.py:187
  273.8 1.1 collective-permute-start.11
  275.0 0.7 bitcast_dynamic-update-slice_fusion.8
  276.3 9.6 %collective-permute-done.8 = bf16[1,32,2048]{2,1,0:T(8,128)(2,1)S(1)} collective-permute-done((bf16[1,32,2048]{2,1,0:T(8,128)(2,1)S(1)}, bf16[1,32,2048]{2,1,0:T(8,128)(2,1)S(1)}, u32[]{:S(2)}, u32[]{:S(2)}) %collective-permute-start.8) | collective-permute-done | bytes 131104 | tf_op jit(solution)/shard_map/ppermute | solution.py:187
  285.9 0.7 bitcast_dynamic-update-slice_fusion.6
  286.6 2.1 collective-permute-done.9
  288.7 1.5 collective-permute-start.14
  290.9 3.3 %collective-permute-done.10 = bf16[1,32,2048]{2,1,0:T(8,128)(2,1)S(1)} collective-permute-done((bf16[1,32,2048]{2,1,0:T(8,128)(2,1)S(1)}, bf16[1,32,2048]{2,1,0:T(8,128)(2,1)S(1)}, u32[]{:S(2)}, u32[]{:S(2)}) %collective-permute-start.10) | collective-permute-done | bytes 131104 | tf_op jit(solution)/shard_map/ppermute | solution.py:187
  294.2 0.7 bitcast_dynamic-update-slice_fusion.4
  294.8 5.3 %collective-permute-done.11 = bf16[1,32,2048]{2,1,0:T(8,128)(2,1)S(1)} collective-permute-done((bf16[1,32,2048]{2,1,0:T(8,128)(2,1)S(1)}, bf16[1,32,2048]{2,1,0:T(8,128)(2,1)S(1)}, u32[]{:S(2)}, u32[]{:S(2)}) %collective-permute-start.11) | collective-permute-done | bytes 131104 | tf_op jit(solution)/shard_map/ppermute | solution.py:187
  300.8 2.5 collective-permute-done.12
  304.0 1.7 collective-permute-done.13
  306.3 2.6 collective-permute-done.14
  308.9 0.7 bitcast_dynamic-update-slice_fusion
  309.6 3.6 %gather_fusion.1 = bf16[16,32,2048]{2,1,0:T(8,128)(2,1)} fusion(bf16[16,32,2048]{2,1,0:T(8,128)(2,1)} %bitcast.184, s32[1024]{0:T(1024)S(1)} %pad_clamp_fusion.1), kind=kCustom, calls=%fused_computation.1 | custom fusion | bytes 4194368 | tf_op jit(solution)/shard_map/gather | solution.py:188
  313.2 4.2 %gather_fusion.2 = bf16[256,2048]{1,0:T(8,128)(2,1)S(1)} fusion(bf16[512,2048]{1,0:T(8,128)(2,1)} %bitcast.180, s32[1024]{0:T(1024)S(1)} %get-tuple-element.39), kind=kCustom, calls=%fused_computation.2 | custom fusion | bytes 2098176 | tf_op jit(solution)/shard_map/gather | solution.py:192
  317.4 1.0 fusion.5
  318.6 0.8 multiply_convert_fusion.2
  (107 shorter events, 13.3 us)
Async XLA Ops:
  6.5 179.2 %copy-start = (bf16[1,384,2048]{2,1,0:T(8,128)(2,1)S(1)}, bf16[1,384,2048]{2,1,0:T(8,128)(2,1)}, u32[]{:S(2)}) copy-start(bf16[1,384,2048]{2,1,0:T(8,128)(2,1)} %param.28) | copy-start | bytes 4718596
  6.5 3.9 %copy-start.1 = (bf16[4,128,512]{2,1,0:T(8,128)(2,1)S(1)}, bf16[4,128,512]{2,1,0:T(8,128)(2,1)}, u32[]{:S(2)}) copy-start(bf16[4,128,512]{2,1,0:T(8,128)(2,1)} %param.17) | copy-start | bytes 1572868
  6.5 71.4 %all-reduce.2.cloned.1.call-start = ((), (), s32[]{:S(2)}) async-start(), calls=%async_computation.2 | async-start | bytes 1048576 | tf_op jit(solution)/shard_map/psum | solution.py:142
  32.6 2.2 slice-start
  32.6 2.2 copy-start.9
  32.6 2.3 slice-start.2
  41.2 0.9 slice-start.1
  41.3 1.0 slice-start.3
  44.2 33.8 %copy-start.3 = (bf16[64,2048]{1,0:T(8,128)(2,1)S(1)}, bf16[64,2048]{1,0:T(8,128)(2,1)}, u32[]{:S(2)}) copy-start(bf16[64,2048]{1,0:T(8,128)(2,1)} %param.20) | copy-start | bytes 786436
  44.2 35.0 %copy-start.6 = (f32[2048]{0:T(1024)S(1)}, f32[2048]{0:T(1024)}, u32[]{:S(2)}) copy-start(f32[2048]{0:T(1024)} %param.22) | copy-start | bytes 24580
  48.1 200.6 %reduce-scatter.2.cloned.1.call-start = ((), (), s32[]{:S(2)}) async-start(), calls=%async_computation.3 | async-start | bytes 6291456 | tf_op jit(solution)/shard_map/reduce_scatter | solution.py:173
  179.6 2.6 copy-start.8
  180.2 2.0 copy-start.2
  195.3 0.7 copy-start.5
  251.2 4.9 %collective-permute-start = (bf16[1,32,2048]{2,1,0:T(8,128)(2,1)}, bf16[1,32,2048]{2,1,0:T(8,128)(2,1)}, u32[]{:S(2)}, u32[]{:S(2)}) collective-permute-start(bf16[1,32,2048]{2,1,0:T(8,128)(2,1)} %get-tuple-element.25), channel_id=1, source_target_pairs={{0,2},{2,0},{4,6},{6,4},{8,10},{10,8},{12,14},{14,12},{16,18},{18,... | collective-permute-start | bytes 393224 | tf_op jit(solution)/shard_map/ppermute | solution.py:187
  252.6 5.3 %collective-permute-start.1 = (bf16[1,32,2048]{2,1,0:T(8,128)(2,1)}, bf16[1,32,2048]{2,1,0:T(8,128)(2,1)S(1)}, u32[]{:S(2)}, u32[]{:S(2)}) collective-permute-start(bf16[1,32,2048]{2,1,0:T(8,128)(2,1)} %get-tuple-element.24), channel_id=1, source_target_pairs={{0,4},{2,6},{4,0},{6,2},{8,12},{10,14},{12,8},{14,10},{16,20},{18,... | collective-permute-start | bytes 393224 | tf_op jit(solution)/shard_map/ppermute | solution.py:187
  252.8 8.3 %collective-permute-start.2 = (bf16[1,32,2048]{2,1,0:T(8,128)(2,1)}, bf16[1,32,2048]{2,1,0:T(8,128)(2,1)S(1)}, u32[]{:S(2)}, u32[]{:S(2)}) collective-permute-start(bf16[1,32,2048]{2,1,0:T(8,128)(2,1)} %get-tuple-element.23), channel_id=1, source_target_pairs={{0,6},{2,4},{4,2},{6,0},{8,14},{10,12},{12,10},{14,8},{16,22},{18,... | collective-permute-start | bytes 393224 | tf_op jit(solution)/shard_map/ppermute | solution.py:187
  254.2 9.7 %collective-permute-start.3 = (bf16[1,32,2048]{2,1,0:T(8,128)(2,1)}, bf16[1,32,2048]{2,1,0:T(8,128)(2,1)S(1)}, u32[]{:S(2)}, u32[]{:S(2)}) collective-permute-start(bf16[1,32,2048]{2,1,0:T(8,128)(2,1)} %get-tuple-element.22), channel_id=1, source_target_pairs={{0,8},{2,10},{4,12},{6,14},{8,0},{10,2},{12,4},{14,6},{16,24},{18,... | collective-permute-start | bytes 393224 | tf_op jit(solution)/shard_map/ppermute | solution.py:187
  254.5 10.5 %collective-permute-start.4 = (bf16[1,32,2048]{2,1,0:T(8,128)(2,1)S(1)}, bf16[1,32,2048]{2,1,0:T(8,128)(2,1)S(1)}, u32[]{:S(2)}, u32[]{:S(2)}) collective-permute-start(bf16[1,32,2048]{2,1,0:T(8,128)(2,1)S(1)} %get-tuple-element.21), channel_id=1, source_target_pairs={{0,10},{2,8},{4,14},{6,12},{8,2},{10,0},{12,6},{14,4},{16,26},{18,... | collective-permute-start | bytes 393224 | tf_op jit(solution)/shard_map/ppermute | solution.py:187
  256.1 11.6 %collective-permute-start.5 = (bf16[1,32,2048]{2,1,0:T(8,128)(2,1)S(1)}, bf16[1,32,2048]{2,1,0:T(8,128)(2,1)S(1)}, u32[]{:S(2)}, u32[]{:S(2)}) collective-permute-start(bf16[1,32,2048]{2,1,0:T(8,128)(2,1)S(1)} %get-tuple-element.20), channel_id=1, source_target_pairs={{0,12},{2,14},{4,8},{6,10},{8,4},{10,6},{12,0},{14,2},{16,28},{18,... | collective-permute-start | bytes 393224 | tf_op jit(solution)/shard_map/ppermute | solution.py:187
  257.9 15.9 %collective-permute-start.6 = (bf16[1,32,2048]{2,1,0:T(8,128)(2,1)S(1)}, bf16[1,32,2048]{2,1,0:T(8,128)(2,1)S(1)}, u32[]{:S(2)}, u32[]{:S(2)}) collective-permute-start(bf16[1,32,2048]{2,1,0:T(8,128)(2,1)S(1)} %get-tuple-element.19), channel_id=1, source_target_pairs={{0,14},{2,12},{4,10},{6,8},{8,6},{10,4},{12,2},{14,0},{16,30},{18,... | collective-permute-start | bytes 393224 | tf_op jit(solution)/shard_map/ppermute | solution.py:187
  261.1 14.5 %collective-permute-start.7 = (bf16[1,32,2048]{2,1,0:T(8,128)(2,1)S(1)}, bf16[1,32,2048]{2,1,0:T(8,128)(2,1)S(1)}, u32[]{:S(2)}, u32[]{:S(2)}) collective-permute-start(bf16[1,32,2048]{2,1,0:T(8,128)(2,1)S(1)} %get-tuple-element.18), channel_id=1, source_target_pairs={{0,16},{2,18},{4,20},{6,22},{8,24},{10,26},{12,28},{14,30},{16,0},... | collective-permute-start | bytes 393224 | tf_op jit(solution)/shard_map/ppermute | solution.py:187
  263.9 22.0 %collective-permute-start.8 = (bf16[1,32,2048]{2,1,0:T(8,128)(2,1)S(1)}, bf16[1,32,2048]{2,1,0:T(8,128)(2,1)S(1)}, u32[]{:S(2)}, u32[]{:S(2)}) collective-permute-start(bf16[1,32,2048]{2,1,0:T(8,128)(2,1)S(1)} %get-tuple-element.17), channel_id=1, source_target_pairs={{0,18},{2,16},{4,22},{6,20},{8,26},{10,24},{12,30},{14,28},{16,2},... | collective-permute-start | bytes 393224 | tf_op jit(solution)/shard_map/ppermute | solution.py:187
  265.0 23.7 %collective-permute-start.9 = (bf16[1,32,2048]{2,1,0:T(8,128)(2,1)S(1)}, bf16[1,32,2048]{2,1,0:T(8,128)(2,1)S(1)}, u32[]{:S(2)}, u32[]{:S(2)}) collective-permute-start(bf16[1,32,2048]{2,1,0:T(8,128)(2,1)S(1)} %get-tuple-element.16), channel_id=1, source_target_pairs={{0,20},{2,22},{4,16},{6,18},{8,28},{10,30},{12,24},{14,26},{16,4},... | collective-permute-start | bytes 393224 | tf_op jit(solution)/shard_map/ppermute | solution.py:187
  267.7 26.5 %collective-permute-start.10 = (bf16[1,32,2048]{2,1,0:T(8,128)(2,1)S(1)}, bf16[1,32,2048]{2,1,0:T(8,128)(2,1)S(1)}, u32[]{:S(2)}, u32[]{:S(2)}) collective-permute-start(bf16[1,32,2048]{2,1,0:T(8,128)(2,1)S(1)} %get-tuple-element.15), channel_id=1, source_target_pairs={{0,22},{2,20},{4,18},{6,16},{8,30},{10,28},{12,26},{14,24},{16,6},... | collective-permute-start | bytes 393224 | tf_op jit(solution)/shard_map/ppermute | solution.py:187
  273.8 26.3 %collective-permute-start.11 = (bf16[1,32,2048]{2,1,0:T(8,128)(2,1)S(1)}, bf16[1,32,2048]{2,1,0:T(8,128)(2,1)S(1)}, u32[]{:S(2)}, u32[]{:S(2)}) collective-permute-start(bf16[1,32,2048]{2,1,0:T(8,128)(2,1)S(1)} %get-tuple-element.14), channel_id=1, source_target_pairs={{0,24},{2,26},{4,28},{6,30},{8,16},{10,18},{12,20},{14,22},{16,8},... | collective-permute-start | bytes 393224 | tf_op jit(solution)/shard_map/ppermute | solution.py:187
  275.6 27.7 %collective-permute-start.12 = (bf16[1,32,2048]{2,1,0:T(8,128)(2,1)S(1)}, bf16[1,32,2048]{2,1,0:T(8,128)(2,1)S(1)}, u32[]{:S(2)}, u32[]{:S(2)}) collective-permute-start(bf16[1,32,2048]{2,1,0:T(8,128)(2,1)S(1)} %get-tuple-element.13), channel_id=1, source_target_pairs={{0,26},{2,24},{4,30},{6,28},{8,18},{10,16},{12,22},{14,20},{16,10}... | collective-permute-start | bytes 393224 | tf_op jit(solution)/shard_map/ppermute | solution.py:187
  285.9 19.8 %collective-permute-start.13 = (bf16[1,32,2048]{2,1,0:T(8,128)(2,1)S(1)}, bf16[1,32,2048]{2,1,0:T(8,128)(2,1)S(1)}, u32[]{:S(2)}, u32[]{:S(2)}) collective-permute-start(bf16[1,32,2048]{2,1,0:T(8,128)(2,1)S(1)} %get-tuple-element.12), channel_id=1, source_target_pairs={{0,28},{2,30},{4,24},{6,26},{8,20},{10,22},{12,16},{14,18},{16,12}... | collective-permute-start | bytes 393224 | tf_op jit(solution)/shard_map/ppermute | solution.py:187
  288.7 20.2 %collective-permute-start.14 = (bf16[1,32,2048]{2,1,0:T(8,128)(2,1)S(1)}, bf16[1,32,2048]{2,1,0:T(8,128)(2,1)S(1)}, u32[]{:S(2)}, u32[]{:S(2)}) collective-permute-start(bf16[1,32,2048]{2,1,0:T(8,128)(2,1)S(1)} %get-tuple-element.11), channel_id=1, source_target_pairs={{0,30},{2,28},{4,26},{6,24},{8,22},{10,20},{12,18},{14,16},{16,14}... | collective-permute-start | bytes 393224 | tf_op jit(solution)/shard_map/ppermute | solution.py:187
  313.2 4.3 %copy-start.4 = (f32[32,8]{1,0:T(8,128)S(1)}, f32[32,8]{1,0:T(8,128)}, u32[]{:S(2)}) copy-start(f32[32,8]{1,0:T(8,128)} %copy.90) | copy-start | bytes 3076
  313.2 5.4 %copy-start.7 = (f32[2048]{0:T(1024)S(1)}, f32[2048]{0:T(1024)}, u32[]{:S(2)}) copy-start(f32[2048]{0:T(1024)} %param.29) | copy-start | bytes 24580
Sparse Core Ops, SparseCore 0:
  48.2 29.6 all-reduce.1
  195.4 53.2 reduce-scatter.1
